TPU v7x, 256 devices: a whole 4x4x8 slice. The times are simulated.
256 devices in a mesh: img: 64 (over x, z, y_lo), txt: 4 (over y_hi, core).
Axes of the slice: x: 4, y: 4 (y_hi: 2, y_lo: 2; y = y_hi * 2 + y_lo), z: 8, core: 2. Of those that a mesh axis runs over, the one named last changes fastest.
Arguments:
- image_tokens: bfloat16 [32768, 256], P(('img', 'txt')), may hold values from -6 to 6
- prompt_tokens: bfloat16 [6144, 256], P(('txt', 'img')), may hold values from -6 to 6
- category_ids: int32 [6144], P(('txt', 'img')), may hold values from 0 to 383, as said below
- prompt_valid: int32 [6144], P(('txt', 'img')), may hold values from 0 to 1, as said below
- image_gain: float32 [256], replicated, may hold values from 0.5 to 1.5
- prompt_gain: float32 [256], replicated, may hold values from 0.5 to 1.5
- query_weight: bfloat16 [256, 1024], replicated, may hold values from -1.7 to 1.7
- key_weight: bfloat16 [256, 1024], replicated, may hold values from -1.7 to 1.7
- image_value_weight: bfloat16 [256, 1024], replicated, may hold values from -0.375 to 0.375
- prompt_value_weight: bfloat16 [256, 1024], replicated, may hold values from -0.375 to 0.375
- image_out_weight: bfloat16 [1024, 256], replicated, may hold values from -0.1875 to 0.1875
- prompt_out_weight: bfloat16 [1024, 256], replicated, may hold values from -0.1875 to 0.1875
- image_layer_scale: float32 [256], replicated, may hold values from 1 to 4
- prompt_layer_scale: float32 [256], replicated, may hold values from 1 to 4
Outputs:
- joined_image: bfloat16 [32768, 256], P(('img', 'txt'))
- joined_prompt: bfloat16 [6144, 256], P(('txt', 'img'))
- category_embed: float32 [384, 256], replicated
Inputs may be any that keep to these rules, and one draw needn't show every extreme that they name: `category_ids`: along the prompt the ids never fall; each of the 384 categories holds between 4 and 28 consecutive tokens. `prompt_valid`: within each category the tokens marked 1 come first, and at least one token is marked 1.
All inputs are finite; a program needn't handle non-finite values.
Results may differ from a plain program's by a relative error of at most 0.009.
The roundings to bfloat16 on the way count: a program that leaves them out, or rounds other values in their place, can miss the bound.
Values may be sent and summed in bfloat16 or wider, within the bound.
No kernel may reach another device: no remote copies, remote signals or barrier semaphores. Data moves between devices by JAX's collectives and lax.ppermute only.
A program may use at most 128 MiB of HBM per device.

v0:
```python
import math
import jax
import jax.numpy as jnp
from jax import lax
from jax.sharding import Mesh
from jax.sharding import PartitionSpec as P

HD = 256
IMG = ("img_0", "img_1", "img_2")
IMG_TXT = ("img_0", "img_1", "img_2", "txt")
TXT_IMG = ("txt", "img_0", "img_1", "img_2")
EPSILON = 1e-05
MASKED = -1e30


def sent_to_all(shard, axis):
    copies = jnp.broadcast_to(shard, (lax.axis_size(axis), *shard.shape))
    return lax.all_to_all(copies, axis, split_axis=0, concat_axis=0, tiled=True)


def in_order(parts, dim):
    parts = jnp.moveaxis(parts, 0, dim)
    lengths = parts.shape
    return parts.reshape(*lengths[:dim], lengths[dim] * lengths[dim + 1], *lengths[dim + 2 :])


def gather_directly(shard, axis, dim):
    parts = sent_to_all(shard, axis)
    return in_order(parts, dim)


def in_one_piece(arrays, axis, dim, along):
    columns = [a.reshape(*a.shape[:along], -1) for a in arrays]
    both = jnp.concatenate(columns, axis=along)
    filled, at, done = (lax.all_gather(both, axis, axis=dim, tiled=True), 0, [])
    for a, column in zip(arrays, columns):
        piece = filled[..., at : at + column.shape[along]]
        done.append(piece.reshape(*piece.shape[:along], *a.shape[along:]))
        at += column.shape[along]
    return tuple(done)


def collected_together(shard, axis):
    leaves = jax.tree.leaves(shard)
    sequence = sorted(range(len(leaves)), key=lambda k: -leaves[k].size)
    width = (1, *leaves[sequence[0]].shape)[-1]
    lines = [
        jnp.pad(leaves[k].reshape(-1), (0, -leaves[k].size % width)).reshape(-1, width)
        for k in sequence
    ]
    both, at, found = (sent_to_all(jnp.concatenate(lines), axis), 0, {})
    for k, line in zip(sequence, lines):
        piece = both[:, at : at + len(line)].reshape(len(both), -1)
        found[k] = piece[:, : leaves[k].size].reshape(-1, *leaves[k].shape)
        at += len(line)
    numbers = iter(range(len(leaves)))
    return jax.tree.map(lambda _: found[next(numbers)], shard)


def joined_by_halves(pieces, combine):
    while len(jax.tree.leaves(pieces)[0]) > 1:
        pieces = jax.vmap(combine)(
            *(jax.tree.map(lambda part: part[side::2], pieces) for side in (0, 1))
        )
    return jax.tree.map(lambda part: part[0], pieces)


def joined_all(shard, axis, combine):
    pieces = collected_together(shard, axis)
    return joined_by_halves(pieces, combine)


def collected_together_2(shard, axis):
    leaves = jax.tree.leaves(shard)
    sequence = sorted(range(len(leaves)), key=lambda k: -leaves[k].size)
    width = (1, *leaves[sequence[0]].shape)[-1]
    lines = [
        jnp.pad(leaves[k].reshape(-1), (0, -leaves[k].size % width)).reshape(-1, width)
        for k in sequence
    ]
    both, at, found = (lax.all_gather(jnp.concatenate(lines), axis), 0, {})
    for k, line in zip(sequence, lines):
        piece = both[:, at : at + len(line)].reshape(len(both), -1)
        found[k] = piece[:, : leaves[k].size].reshape(-1, *leaves[k].shape)
        at += len(line)
    numbers = iter(range(len(leaves)))
    return jax.tree.map(lambda _: found[next(numbers)], shard)


def joined_all_2(shard, axes, combine):
    for axis in axes:
        pieces = collected_together_2(shard, axis)
        shard = jax.tree.map(lambda part: part[0], pieces)
        for k in range(1, lax.axis_size(axis)):
            shard = combine(shard, jax.tree.map(lambda part: part[k], pieces))
    return shard


def cut_along(shard, dim, size):
    lengths = shard.shape
    parts = shard.reshape(*lengths[:dim], size, lengths[dim] // size, *lengths[dim + 1 :])
    return jnp.moveaxis(parts, dim, 0)


def sent_and_summed(shard, axis, dim):
    size = lax.axis_size(axis)
    parts = lax.all_to_all(cut_along(shard, dim, size), axis, 0, 0, tiled=True)
    return jnp.sum(parts.astype(jnp.float32), axis=0)


def sent_and_summed_2(shard, axis, dim):
    parts = cut_along(shard, dim, lax.axis_size(axis))
    arrived = lax.all_to_all(parts, axis, split_axis=0, concat_axis=0, tiled=True)
    return arrived.sum(axis=0)


def together(arrays, axis):
    ravelled, at, done = (jnp.concatenate([a.reshape(-1) for a in arrays]), 0, [])
    total = lax.psum(ravelled, axis)
    for a in arrays:
        done.append(total[at : at + a.size].reshape(a.shape))
        at += a.size
    return tuple(done)


def normalize(tokens_in, gain_row):
    values = tokens_in.astype(jnp.float32)
    average = jnp.mean(values, axis=-1, keepdims=True)
    centered = values - average
    variance = jnp.mean(centered * centered, axis=-1, keepdims=True)
    return (centered * lax.rsqrt(variance + EPSILON) * gain_row).astype(jnp.bfloat16)


def combine_stats(left_stats, right_stats):
    highest = jnp.maximum(left_stats[0], right_stats[0])
    summed = left_stats[1] * jnp.exp(left_stats[0] - highest) + right_stats[1] * jnp.exp(
        right_stats[0] - highest
    )
    return (highest, summed)


def on_device(
    image_tokens,
    prompt_tokens,
    category_ids,
    prompt_valid,
    image_gain,
    prompt_gain,
    query_weight,
    key_weight,
    image_value_weight,
    prompt_value_weight,
    image_out_weight,
    prompt_out_weight,
    image_layer_scale,
    prompt_layer_scale,
):
    embed_width = query_weight.shape[1]
    head_count = embed_width // HD
    image_normed = normalize(image_tokens, image_gain)
    image_weights = jnp.concatenate([query_weight, image_value_weight], axis=1)
    image_projected = jnp.dot(
        gather_directly(image_normed, "txt", 0), image_weights, preferred_element_type=jnp.float32
    ).astype(jnp.bfloat16)
    prompt_normed = normalize(prompt_tokens, prompt_gain)
    prompt_weights = jnp.concatenate([key_weight, prompt_value_weight], axis=1)
    valid_marks = prompt_valid.astype(jnp.bfloat16)
    gathered, marks_all = in_one_piece((prompt_normed, valid_marks), IMG, 0, 1)
    prompt_projected = jnp.dot(gathered, prompt_weights, preferred_element_type=jnp.float32).astype(
        jnp.bfloat16
    )
    image_count = image_projected.shape[0]
    prompt_count = prompt_projected.shape[0]
    query_heads = image_projected[:, :embed_width].reshape(image_count, head_count, HD)
    image_value_heads = image_projected[:, embed_width:].reshape(image_count, head_count, HD)
    key_heads = prompt_projected[:, :embed_width].reshape(prompt_count, head_count, HD)
    prompt_value_heads = prompt_projected[:, embed_width:].reshape(prompt_count, head_count, HD)
    scores = jnp.einsum(
        "ihd,thd->hit", query_heads, key_heads, preferred_element_type=jnp.float32
    ) / math.sqrt(HD)
    is_valid = (marks_all > 0)[None, None, :]
    masked = jnp.where(is_valid, scores, MASKED)
    local_row_top = jnp.max(masked, axis=2)
    local_row_sum = jnp.sum(
        jnp.where(is_valid, jnp.exp(masked - local_row_top[:, :, None]), 0.0), axis=2
    )
    row_top, row_sum = joined_all((local_row_top, local_row_sum), "txt", combine_stats)
    local_col_top = jnp.max(scores, axis=1)
    local_col_sum = jnp.sum(jnp.exp(scores - local_col_top[:, None, :]), axis=1)
    col_top, col_sum = joined_all_2((local_col_top, local_col_sum), IMG, combine_stats)
    row_weights = jnp.where(is_valid, jnp.exp(masked - row_top[:, :, None]), 0.0).astype(
        jnp.bfloat16
    )
    col_weights = jnp.exp(scores - col_top[:, None, :]).astype(jnp.bfloat16)
    image_numer = jnp.einsum(
        "hit,thd->ihd", row_weights, prompt_value_heads, preferred_element_type=jnp.float32
    )
    image_part = (
        (image_numer / row_sum.T[:, :, None]).reshape(image_count, embed_width).astype(jnp.bfloat16)
    )
    block_rows = image_part
    image_delta = sent_and_summed(
        jnp.dot(block_rows, image_out_weight, preferred_element_type=jnp.float32).astype(
            jnp.bfloat16
        ),
        "txt",
        0,
    )
    joined_image = (image_tokens.astype(jnp.float32) + image_layer_scale * image_delta).astype(
        jnp.bfloat16
    )
    prompt_numer = jnp.einsum(
        "hit,ihd->thd", col_weights, image_value_heads, preferred_element_type=jnp.float32
    )
    prompt_part = (
        (prompt_numer / col_sum.T[:, :, None])
        .reshape(prompt_count, embed_width)
        .astype(jnp.bfloat16)
    )
    block_rows = prompt_part
    prompt_delta = sent_and_summed_2(
        jnp.dot(block_rows, prompt_out_weight, preferred_element_type=jnp.float32), IMG, 0
    )
    prompt_joined = prompt_tokens.astype(jnp.float32) + prompt_layer_scale * prompt_delta
    category_count = prompt_count * lax.axis_size("txt") // 16
    members = jnp.logical_and(
        category_ids[None, :] == jnp.arange(category_count, dtype=jnp.int32)[:, None],
        prompt_valid[None, :] > 0,
    ).astype(jnp.float32)
    category_sum = jnp.dot(members, prompt_joined)
    category_tally = jnp.sum(members, axis=1)
    category_sum, category_tally = together((category_sum, category_tally), IMG_TXT)
    category_embed = category_sum / category_tally[:, None]
    return (joined_image, prompt_joined.astype(jnp.bfloat16), category_embed)


def solution(mesh):
    finer = Mesh(
        mesh.devices.reshape(4, 8, 2, mesh.shape["txt"]), ("img_0", "img_1", "img_2", "txt")
    )
    return jax.shard_map(
        on_device,
        mesh=finer,
        in_specs=(
            P(IMG_TXT, None),
            P(TXT_IMG, None),
            P(TXT_IMG),
            P(TXT_IMG),
            P(),
            P(),
            P(),
            P(),
            P(),
            P(),
            P(),
            P(),
            P(),
            P(),
        ),
        out_specs=(P(IMG_TXT, None), P(TXT_IMG, None), P()),
        check_vma=False,
    )
```

profile of v0, /device:TPU:1, one launch (start us, length us, event | category | flops | bytes accessed | tf_op | source)
XLA Modules:
  0.0 599.6 jit_solution(7328133230477263510)
XLA Ops:
  7.2 1.0 convert_reduce_fusion.1
  8.2 1.0 fusion.23
  9.2 1.0 fusion.25
  10.9 6.6 %all-to-all-start = ((bf16[4,128,256]{2,1,0:T(8,128)(2,1)}), bf16[4,128,256]{2,1,0:T(8,128)(2,1)S(1)}, u32[]{:S(2)}, u32[]{:S(2)}) async-start(bf16[4,128,256]{2,1,0:T(8,128)(2,1)} %broadcast_in_dim.27), calls=%async_computation | async-start | bytes 524288 | tf_op jit(solution)/shard_map/all_to_all | solution.py:18
  18.2 0.8 convert_reduce_fusion.2
  19.1 0.9 fusion.31
  20.0 0.8 fusion.33
  20.8 136.4 %all_gather.21 = bf16[1536,257]{1,0:T(8,128)(2,1)S(1)} all-gather(bf16[24,257]{1,0:T(8,128)(2,1)S(1)} %pad_maximum_fusion.4), channel_id=1, replica_groups=mesh['img_0'=4,'img_1'=8,'img_2'=2,'txt'=4] {'img_0','img_1','img_2'}, dimensions={0}, use_global_device_ids=true | all-gather | bytes 801840 | tf_op jit(solution)/shard_map/all_gather | solution.py:35
  157.2 3.0 convolution_convert_fusion
  160.2 3.5 fusion.94
  163.8 4.8 copy.35
  169.8 1.0 copy-done.2
  170.7 2.5 multiply_reduce_fusion
  173.3 5.3 exponential_reduce_fusion
  179.3 32.9 %all-to-all-start.1 = ((f32[4,8,512]{2,1,0:T(8,128)}), f32[4,8,512]{2,1,0:T(8,128)S(1)}, u32[]{:S(2)}, u32[]{:S(2)}) async-start(f32[4,8,512]{2,1,0:T(8,128)} %broadcast_in_dim.50), calls=%async_computation.1 | async-start | bytes 131072 | tf_op jit(solution)/shard_map/all_to_all | solution.py:18
  212.1 9.5 %all-gather = f32[32,1536]{1,0:T(8,128)S(1)} all-gather(f32[8,1536]{1,0:T(8,128)S(1)} %pad_maximum_fusion.1), channel_id=2, replica_groups=mesh['img_0'=4,'img_1'=8,'img_2'=2,'txt'=4] {'img_0'}, dimensions={0}, use_global_device_ids=true | all-gather | bytes 245760 | tf_op jit(solution)/shard_map/all_gather | solution.py:81
  221.8 19.3 %all-gather.1 = f32[64,1536]{1,0:T(8,128)S(1)} all-gather(f32[8,1536]{1,0:T(8,128)S(1)} %pad_maximum_fusion.2), channel_id=3, replica_groups=mesh['img_0'=4,'img_1'=8,'img_2'=2,'txt'=4] {'img_1'}, dimensions={0}, use_global_device_ids=true | all-gather | bytes 442368 | tf_op jit(solution)/shard_map/all_gather | solution.py:81
  241.3 3.8 all-gather.2
  245.7 9.1 %fusion.1 = bf16[1536,4,256]{0,2,1:T(8,128)(2,1)} fusion(f32[1536,4]{0,1:T(4,128)S(1)} %get-tuple-element.7, bf16[512,4,256]{0,2,1:T(8,128)(2,1)S(1)} %bitcast.311, f32[4,512,1536]{2,1,0:T(8,128)} %copy-done.1, f32[4,1536]{1,0:T(4,128)S(1)} %get-tuple-element.8), kind=kOutput, calls=%fused_computation.9 | convolution fusion | flops 1623195648 | bytes 16826368 | tf_op jit(solution)/shard_map/hit,ihd->thd/dot_general | solution.py:212
  254.7 5.9 copy.34
  260.6 6.1 %convert_element_type.72 = bf16[64,24,1024]{2,1,0:T(8,128)(2,1)} reshape(bf16[1536,4,256]{2,1,0:T(4,128)(2,1)} %copy.34) | data formatting | bytes 6291456 | tf_op jit(solution)/shard_map/convert_element_type | solution.py:218
  266.8 8.7 %fusion.9 = bf16[512,4,256]{0,2,1:T(8,128)(2,1)S(1)} fusion(bf16[1536,4,256]{0,2,1:T(8,128)(2,1)} %bitcast.306, f32[4,512,1536]{2,1,0:T(8,128)} %copy-done.1, f32[4,512]{1,0:T(4,128)S(1)} %get-tuple-element.22, pred[1536]{0:T(1024)(128)(4,1)S(1)} %compare_reduce_fusion, f32[512,4]{0,1:T(4,128)S(1)} %get-tuple-element.21), kind=kOutput, calls=%fused_computation.19 | convolution fusion | flops 1627389952 | bytes 16795136 | tf_op jit(solution)/shard_map/hit,thd->ihd/dot_general | solution.py:195
  275.6 1.2 convolution_convert_fusion.2
  276.8 14.4 %all-to-all-start.2 = ((bf16[4,128,256]{2,1,0:T(8,128)(2,1)}), bf16[4,128,256]{2,1,0:T(8,128)(2,1)S(1)}, u32[]{:S(2)}, u32[]{:S(2)}) async-start(bf16[4,128,256]{2,1,0:T(8,128)(2,1)} %bitcast.8), calls=%async_computation.2 | async-start | bytes 524288 | tf_op jit(solution)/shard_map/all_to_all | solution.py:107
  291.2 4.0 fusion.19
  295.2 2.5 all-to-all-done.2
  297.7 4.7 all-to-all-start.3
  303.3 37.4 %all-to-all-done.3 = f32[64,24,256]{2,1,0:T(8,128)S(1)} async-done(((f32[64,24,256]{2,1,0:T(8,128)}), f32[64,24,256]{2,1,0:T(8,128)S(1)}, u32[]{:S(2)}, u32[]{:S(2)}) %all-to-all-start.3) | async-done | bytes 1572896 | tf_op jit(solution)/shard_map/all_to_all | solution.py:113
  341.4 0.8 pad_maximum_fusion
  342.8 247.2 %all-reduce.2.cloned.1.call-done = f32[98688]{0:T(1024)} async-done(((f32[98688]{0:T(1024)}), f32[98688]{0:T(1024)}) %all-reduce.2.cloned.1.call-update) | async-done | bytes 394768 | tf_op jit(solution)/shard_map/psum | solution.py:119
  590.1 1.0 slice.262
  591.9 0.9 broadcast_divide_fusion
  (60 shorter events, 7.2 us)
Async XLA Ops:
  7.2 284.0 %copy-start = (bf16[1024,256]{1,0:T(8,128)(2,1)S(1)}, bf16[1024,256]{1,0:T(8,128)(2,1)}, u32[]{:S(2)}) copy-start(bf16[1024,256]{1,0:T(8,128)(2,1)} %param.25) | copy-start | bytes 1572868
  10.9 157.9 %all-to-all-start = ((bf16[4,128,256]{2,1,0:T(8,128)(2,1)}), bf16[4,128,256]{2,1,0:T(8,128)(2,1)S(1)}, u32[]{:S(2)}, u32[]{:S(2)}) async-start(bf16[4,128,256]{2,1,0:T(8,128)(2,1)} %broadcast_in_dim.27), calls=%async_computation | async-start | bytes 524288 | tf_op jit(solution)/shard_map/all_to_all | solution.py:18
  163.8 5.1 copy-start.4
  163.8 5.1 copy-start.5
  168.9 1.9 copy-start.2
  173.3 5.3 copy-start.1
  179.3 87.5 %all-to-all-start.1 = ((f32[4,8,512]{2,1,0:T(8,128)}), f32[4,8,512]{2,1,0:T(8,128)S(1)}, u32[]{:S(2)}, u32[]{:S(2)}) async-start(f32[4,8,512]{2,1,0:T(8,128)} %broadcast_in_dim.50), calls=%async_computation.1 | async-start | bytes 131072 | tf_op jit(solution)/shard_map/all_to_all | solution.py:18
  266.8 8.8 %copy-start.10 = (bf16[1024,256]{1,0:T(8,128)(2,1)S(1)}, bf16[1024,256]{1,0:T(8,128)(2,1)}, u32[]{:S(2)}) copy-start(bf16[1024,256]{1,0:T(8,128)(2,1)} %param.24) | copy-start | bytes 1572868
  275.5 26.9 %copy-start.11 = (s32[24]{0:T(128)S(1)}, s32[24]{0:T(128)}, u32[]{:S(2)}) copy-start(s32[24]{0:T(128)} %param.17) | copy-start | bytes 292
  275.5 27.0 %copy-start.8 = (s32[24]{0:T(128)S(1)}, s32[24]{0:T(128)}, u32[]{:S(2)}) copy-start(s32[24]{0:T(128)} %param.16) | copy-start | bytes 292
  275.5 27.1 %copy-start.3 = (bf16[128,256]{1,0:T(8,128)(2,1)S(1)}, bf16[128,256]{1,0:T(8,128)(2,1)}, u32[]{:S(2)}) copy-start(bf16[128,256]{1,0:T(8,128)(2,1)} %param.14) | copy-start | bytes 196612
  275.6 27.1 %copy-start.9 = (f32[256]{0:T(256)S(1)}, f32[256]{0:T(256)}, u32[]{:S(2)}) copy-start(f32[256]{0:T(256)} %param.26) | copy-start | bytes 3076
  275.6 65.3 %copy-start.6 = (bf16[24,256]{1,0:T(8,128)(2,1)S(1)}, bf16[24,256]{1,0:T(8,128)(2,1)}, u32[]{:S(2)}) copy-start(bf16[24,256]{1,0:T(8,128)(2,1)} %param.15) | copy-start | bytes 36868
  275.6 65.3 %copy-start.7 = (f32[256]{0:T(256)S(1)}, f32[256]{0:T(256)}, u32[]{:S(2)}) copy-start(f32[256]{0:T(256)} %param.27) | copy-start | bytes 3076
  276.8 20.9 %all-to-all-start.2 = ((bf16[4,128,256]{2,1,0:T(8,128)(2,1)}), bf16[4,128,256]{2,1,0:T(8,128)(2,1)S(1)}, u32[]{:S(2)}, u32[]{:S(2)}) async-start(bf16[4,128,256]{2,1,0:T(8,128)(2,1)} %bitcast.8), calls=%async_computation.2 | async-start | bytes 524288 | tf_op jit(solution)/shard_map/all_to_all | solution.py:107
  297.7 43.0 %all-to-all-start.3 = ((f32[64,24,256]{2,1,0:T(8,128)}), f32[64,24,256]{2,1,0:T(8,128)S(1)}, u32[]{:S(2)}, u32[]{:S(2)}) async-start(f32[64,24,256]{2,1,0:T(8,128)} %fusion.19), calls=%async_computation.3 | async-start | bytes 3145728 | tf_op jit(solution)/shard_map/all_to_all | solution.py:113
  302.4 287.7 %all-reduce.2.cloned.1.call-start = ((), (), s32[]{:S(2)}) async-start(), calls=%async_computation.4 | async-start | bytes 794624 | tf_op jit(solution)/shard_map/psum | solution.py:119
Sparse Core Ops, SparseCore 0:
  342.3 247.6 all-reduce.1
where the time goes:
time: 601 us; the launch traced here: 600 us
  waiting for transfers between devices  287 us (48%)
  blocking collectives  169 us (28%)
  starting transfers between devices  58.5 us (10%)
  matrix products  29.6 us (5%)
  local copies, waits for them, and re-layouts  25.5 us (4%)
  other arithmetic  15.3 us (3%)
  between operations  14.4 us (2%)
    psum x1, waiting for transfers between devices, together(): total = lax.psum(ravelled, axis)  247 us
    all_gather x1, blocking collectives, in_one_piece(): filled, at, done = (lax.all_gather(both, axis, axis=dim, tiled=True), 0, [])  136 us
    all_to_all x2, starting transfers between devices, sent_to_all(): return lax.all_to_all(copies, axis, split_axis=0, concat_axis=0, tiled=True)  39.4 us
    all_to_all x1, waiting for transfers between devices, sent_and_summed_2(): lax.all_to_all(parts, axis, split_axis=0, concat_axis=0, tiled=True)  37.4 us
    all_gather x3, blocking collectives, collected_together_2(): both, at, found = (lax.all_gather(jnp.concatenate(lines), axis), 0, {})  32.7 us
    all_to_all x1, starting transfers between devices, sent_and_summed(): parts = lax.all_to_all(cut_along(shard, dim, size), axis, 0, 0, tiled=True)  14.4 us
  transfers between devices with their start and end apart: 5, of which 3 were waited for; matrix products, arithmetic and copies ran while one was open for 7% of the time, Pallas kernels for 0%

commit v1 on v0

--- a/solution.py
+++ b/solution.py
@@ -116,7 +116,7 @@
 
 def together(arrays, axis):
     ravelled, at, done = (jnp.concatenate([a.reshape(-1) for a in arrays]), 0, [])
-    total = lax.psum(ravelled, axis)
+    total = jnp.sum(lax.all_gather(ravelled, axis), axis=0)
     for a in arrays:
         done.append(total[at : at + a.size].reshape(a.shape))
         at += a.size

time: 601 us -> 943 us (1.57)
  waiting for transfers between devices: 287 us -> 541 us
  other arithmetic: 15.3 us -> 93 us
  blocking collectives: 169 us -> 183 us
    all_gather x0 -> x1, waiting for transfers between devices: none -> 518 us  [together(): total = jnp.sum(lax.all_gather(ravelled, axis), axis=0)]
    psum x1 -> x0, waiting for transfers between devices: 247 us -> none  [together(): total = lax.psum(ravelled, axis)]
    reduce_sum x0 -> x1, other arithmetic: none -> 78.6 us  [together(): total = jnp.sum(lax.all_gather(ravelled, axis), axis=0)]
    all_to_all x1 -> x0, starting transfers between devices: 14.4 us -> none  [sent_and_summed(): parts = lax.all_to_all(cut_along(shard, dim, size), axis, 0, 0, tiled=True)]
    all_to_all x0 -> x1, blocking collectives: none -> 14.3 us  [sent_and_summed(): parts = lax.all_to_all(cut_along(shard, dim, size), axis, 0, 0, tiled=True)]
    all_to_all x1, waiting for transfers between devices: 37.4 us -> 23.6 us  [sent_and_summed_2(): lax.all_to_all(parts, axis, split_axis=0, concat_axis=0, tiled=True)]
    all_to_all x2, starting transfers between devices: 39.4 us -> 52.7 us  [sent_to_all(): return lax.all_to_all(copies, axis, split_axis=0, concat_axis=0, tiled=True)]
  transfers between devices with their start and end apart: 5 -> 4, of which waited for: 3 -> 3; matrix products, arithmetic and copies ran while one was open for 7% -> 3% of each run, Pallas kernels for 0% -> 0%
where the time goes in v1:
time: 943 us; the launch traced here: 940 us
  waiting for transfers between devices  541 us (57%)
  blocking collectives  183 us (19%)
  other arithmetic  93 us (10%)
  starting transfers between devices  57.6 us (6%)
  matrix products  26.5 us (3%)
  local copies, waits for them, and re-layouts  24.8 us (3%)
  between operations  14.4 us (2%)
    all_gather x1, waiting for transfers between devices, together(): total = jnp.sum(lax.all_gather(ravelled, axis), axis=0)  518 us
    all_gather x1, blocking collectives, in_one_piece(): filled, at, done = (lax.all_gather(both, axis, axis=dim, tiled=True), 0, [])  136 us
    reduce_sum x1, other arithmetic, together(): total = jnp.sum(lax.all_gather(ravelled, axis), axis=0)  78.6 us
    all_to_all x2, starting transfers between devices, sent_to_all(): return lax.all_to_all(copies, axis, split_axis=0, concat_axis=0, tiled=True)  52.7 us
    all_gather x3, blocking collectives, collected_together_2(): both, at, found = (lax.all_gather(jnp.concatenate(lines), axis), 0, {})  32.1 us
    all_to_all x1, waiting for transfers between devices, sent_and_summed_2(): lax.all_to_all(parts, axis, split_axis=0, concat_axis=0, tiled=True)  23.6 us
  transfers between devices with their start and end apart: 4, of which 3 were waited for; matrix products, arithmetic and copies ran while one was open for 3% of the time, Pallas kernels for 0%

profile of v1, /device:TPU:1, one launch (start us, length us, event | category | flops | bytes accessed | tf_op | source)
XLA Modules:
  0.0 940.4 jit_solution(12281712484947794744)
XLA Ops:
  7.2 1.0 convert_reduce_fusion.1
  8.2 1.0 fusion.23
  9.2 1.0 fusion.25
  10.2 0.7 broadcast_in_dim.27
  10.9 6.6 all-to-all-start
  18.1 0.8 convert_reduce_fusion.2
  19.0 0.9 fusion.31
  20.0 0.8 fusion.33
  20.8 136.4 %all_gather.27 = bf16[1536,257]{1,0:T(8,128)(2,1)S(1)} all-gather(bf16[24,257]{1,0:T(8,128)(2,1)S(1)} %pad_maximum_fusion.4), channel_id=1, replica_groups=mesh['img_0'=4,'img_1'=8,'img_2'=2,'txt'=4] {'img_0','img_1','img_2'}, dimensions={0}, use_global_device_ids=true | all-gather | bytes 801840 | tf_op jit(solution)/shard_map/all_gather | solution.py:35
  157.2 3.0 convolution_convert_fusion
  160.3 3.5 fusion.94
  164.1 0.7 convolution_convert_fusion.1
  164.8 1.2 fusion.95
  166.5 4.7 multiply_reduce_fusion
  171.2 5.3 exponential_reduce_fusion
  176.5 9.2 all-gather
  185.9 18.9 %all-gather.1 = f32[64,1536]{1,0:T(8,128)S(1)} all-gather(f32[8,1536]{1,0:T(8,128)S(1)} %pad_maximum_fusion.2), channel_id=3, replica_groups=mesh['img_0'=4,'img_1'=8,'img_2'=2,'txt'=4] {'img_1'}, dimensions={0}, use_global_device_ids=true | all-gather | bytes 442368 | tf_op jit(solution)/shard_map/all_gather | solution.py:81
  205.0 3.9 all-gather.2
  208.9 4.2 fusion.1
  213.1 5.9 copy.40
  219.0 6.1 convert_element_type.72
  225.1 4.1 fusion.19
  229.2 4.9 all-to-all-start.3
  234.2 23.6 %all-to-all-done.3 = f32[64,24,256]{2,1,0:T(8,128)S(1)} async-done(((f32[64,24,256]{2,1,0:T(8,128)}), f32[64,24,256]{2,1,0:T(8,128)S(1)}, u32[]{:S(2)}, u32[]{:S(2)}) %all-to-all-start.3) | async-done | bytes 1572896 | tf_op jit(solution)/shard_map/all_to_all | solution.py:113
  258.6 1.0 reshape.123
  260.3 46.1 %all-to-all-start.1 = ((f32[4,8,512]{2,1,0:T(8,128)}), f32[4,8,512]{2,1,0:T(8,128)S(1)}, u32[]{:S(2)}, u32[]{:S(2)}) async-start(f32[4,8,512]{2,1,0:T(8,128)} %broadcast_in_dim.50), calls=%async_computation.1 | async-start | bytes 131072 | tf_op jit(solution)/shard_map/all_to_all | solution.py:18
  306.4 4.7 copy.41
  311.2 9.0 fusion.9
  320.8 14.3 %all_to_all.20 = bf16[4,128,256]{2,1,0:T(8,128)(2,1)S(1)} all-to-all(bf16[4,128,256]{2,1,0:T(8,128)(2,1)S(1)} %bitcast.315), channel_id=1, replica_groups=mesh['img_0'=4,'img_1'=8,'img_2'=2,'txt'=4] {'txt'}, dimensions={0} | all-to-all | bytes 524288 | tf_op jit(solution)/shard_map/all_to_all | solution.py:107
  336.4 517.5 %all-gather.7.cloned.1.call-done = f32[256,1,98688]{2,1,0:T(1,128)} async-done(((f32[1,1,98688]{2,1,0:T(1,128)}), f32[256,1,98688]{2,1,0:T(1,128)}) %all-gather.7.cloned.1.call-update) | async-done | bytes 101056528 | tf_op jit(solution)/shard_map/all_gather | solution.py:119
  853.9 78.6 %reduce_sum.99 = f32[98688]{0:T(1024)S(1)} reduce(f32[256,1,98688]{2,1,0:T(1,128)} %all-gather.7.cloned.1.call-done, f32[]{:T(128)} %constant.8.clone.1), dimensions={0,1}, to_apply=%region_11.12 | reduce | flops 25165440 | bytes 101451264 | tf_op jit(solution)/shard_map/reduce_sum | solution.py:119
  932.6 0.9 broadcast_divide_fusion
  (59 shorter events, 5.5 us)
Async XLA Ops:
  7.2 218.0 %copy-start = (bf16[1024,256]{1,0:T(8,128)(2,1)S(1)}, bf16[1024,256]{1,0:T(8,128)(2,1)}, u32[]{:S(2)}) copy-start(bf16[1024,256]{1,0:T(8,128)(2,1)} %param.25) | copy-start | bytes 1572868
  10.9 153.1 %all-to-all-start = ((bf16[4,128,256]{2,1,0:T(8,128)(2,1)}), bf16[4,128,256]{2,1,0:T(8,128)(2,1)S(1)}, u32[]{:S(2)}, u32[]{:S(2)}) async-start(bf16[4,128,256]{2,1,0:T(8,128)(2,1)} %broadcast_in_dim.27), calls=%async_computation | async-start | bytes 524288 | tf_op jit(solution)/shard_map/all_to_all | solution.py:18
  160.2 3.8 copy-start.3
  160.2 3.8 copy-start.4
  171.2 37.7 %copy-start.1 = (f32[4,512,1536]{2,1,0:T(8,128)}, f32[4,512,1536]{2,1,0:T(8,128)S(1)}, u32[]{:S(2)}) copy-start(f32[4,512,1536]{2,1,0:T(8,128)S(1)} %get-tuple-element.23) | copy-start | bytes 37748740
  219.0 15.1 %copy-start.10 = (s32[24]{0:T(128)S(1)}, s32[24]{0:T(128)}, u32[]{:S(2)}) copy-start(s32[24]{0:T(128)} %param.17) | copy-start | bytes 292
  219.0 15.1 %copy-start.7 = (s32[24]{0:T(128)S(1)}, s32[24]{0:T(128)}, u32[]{:S(2)}) copy-start(s32[24]{0:T(128)} %param.16) | copy-start | bytes 292
  225.1 32.8 %copy-start.5 = (bf16[24,256]{1,0:T(8,128)(2,1)S(1)}, bf16[24,256]{1,0:T(8,128)(2,1)}, u32[]{:S(2)}) copy-start(bf16[24,256]{1,0:T(8,128)(2,1)} %param.15) | copy-start | bytes 36868
  225.1 32.8 %copy-start.6 = (f32[256]{0:T(256)S(1)}, f32[256]{0:T(256)}, u32[]{:S(2)}) copy-start(f32[256]{0:T(256)} %param.27) | copy-start | bytes 3076
  229.2 28.6 %all-to-all-start.3 = ((f32[64,24,256]{2,1,0:T(8,128)}), f32[64,24,256]{2,1,0:T(8,128)S(1)}, u32[]{:S(2)}, u32[]{:S(2)}) async-start(f32[64,24,256]{2,1,0:T(8,128)} %fusion.19), calls=%async_computation.3 | async-start | bytes 3145728 | tf_op jit(solution)/shard_map/all_to_all | solution.py:113
  234.1 619.9 %all-gather.7.cloned.1.call-start = ((), (), s32[]{:S(2)}) async-start(), calls=%async_computation.4 | async-start | bytes 101451264 | tf_op jit(solution)/shard_map/all_gather | solution.py:119
  260.3 50.9 %all-to-all-start.1 = ((f32[4,8,512]{2,1,0:T(8,128)}), f32[4,8,512]{2,1,0:T(8,128)S(1)}, u32[]{:S(2)}, u32[]{:S(2)}) async-start(f32[4,8,512]{2,1,0:T(8,128)} %broadcast_in_dim.50), calls=%async_computation.1 | async-start | bytes 131072 | tf_op jit(solution)/shard_map/all_to_all | solution.py:18
  311.2 9.1 copy-start.9
  311.2 23.9 %copy-start.2 = (bf16[128,256]{1,0:T(8,128)(2,1)S(1)}, bf16[128,256]{1,0:T(8,128)(2,1)}, u32[]{:S(2)}) copy-start(bf16[128,256]{1,0:T(8,128)(2,1)} %param.14) | copy-start | bytes 196612
  311.2 23.9 %copy-start.8 = (f32[256]{0:T(256)S(1)}, f32[256]{0:T(256)}, u32[]{:S(2)}) copy-start(f32[256]{0:T(256)} %param.26) | copy-start | bytes 3076
Sparse Core Ops, SparseCore 0:
  259.7 594.1 all-gather.6
